TPU v7x, 32 devices: a whole 2x2x4 slice. The times are simulated.
32 devices in a mesh: dom: 4 (over y, x), sep: 8 (over z, core).
Axes of the slice: x: 2, y: 2, z: 4, core: 2. Of those that a mesh axis runs over, the one named last changes fastest.
Arguments:
- rhs_leaf: bfloat16 [4, 4096, 1536], P('dom', 'sep'), may hold values from -6 to 6
- rhs_middle: bfloat16 [4, 4096, 768], P('dom', 'sep'), may hold values from -6 to 6
- rhs_top: bfloat16 [4, 4096, 384], P('dom', 'sep'), may hold values from -6 to 6
- update_leaf: bfloat16 [4, 4096, 256], P('dom', 'sep'), may hold values from -0.375 to 0.375
- couple_leaf: bfloat16 [4, 4096, 256], P('dom', 'sep'), may hold values from -0.09375 to 0.09375
- update_middle: bfloat16 [4, 4096, 256], P('dom', 'sep'), may hold values from -0.375 to 0.375, as said below
- couple_middle: bfloat16 [4, 4096, 256], P('dom', 'sep'), may hold values from -0.09375 to 0.09375, as said below
- pivot_leaf: float32 [4, 4096], P('dom', 'sep'), may hold values from 2.2 to 4
- pivot_middle: float32 [2, 4096], P(None, 'sep'), may hold values from 2.2 to 4
- pivot_top: float32 [1, 4096], P(None, 'sep'), may hold values from 2.2 to 4
- front_rows: int32 [4, 8], P('dom', 'sep'), may hold values from 128 to 512, as said below
- rank_leaf: int32 [4], P('dom'), may hold values from 64 to 256, as said below
- rank_middle: int32 [2], replicated, may hold values from 64 to 256, as said below
Outputs:
- top_values: float32 [4, 4096, 384], P('dom', 'sep')
Inputs may be any that keep to these rules, and one draw needn't show every extreme that they name: `front_rows`: in every draw some front has all 512 rows of some row block live. `rank_leaf`: some leaf front has rank 256 in every draw. `rank_middle`: some middle front has rank 256 in every draw. `update_middle`: rows 2g and 2g+1 are equal; entries lie within plus or minus 6 / sqrt(256). `couple_middle`: rows 2g and 2g+1 are equal; entries lie within plus or minus 6 / sqrt(4096).
All inputs are finite; a program needn't handle non-finite values.
Results may differ from a plain program's by a relative error of at most 0.0018.
Values may be sent and summed in bfloat16 or wider, within the bound.
A program may use at most 64 MiB of HBM per device.

v0:
```python
import functools

import jax
import jax.numpy as jnp
from jax import lax
from jax.experimental import pallas as pl
from jax.experimental.pallas import tpu as pltpu
from jax.sharding import PartitionSpec as P

MESH = pl.DeviceIdType.MESH
F32 = jnp.float32
BF16 = jnp.bfloat16
CW = 128
HOP = 5
LAG = 3
LAND = 4


def flipped(value, bit):
    return value + bit - 2 * bit * (lax.rem(value // bit, 2))


def spread(row, height):
    return jnp.broadcast_to(row, (height, row.shape[1])).T


def kernel(
    n_sep,
    rhs_leaf, rhs_middle, rhs_top, update_leaf, couple_leaf, update_middle, couple_middle,
    pivot_leaf, pivot_middle, pivot_top, front_rows_hbm, rank_leaf_hbm, rank_middle_hbm,
    out,
    front_rows, rank_leaf, rank_middle, pivot_v,
    leaf_v, middle_v, top_v, couple_v, factor_leaf, factor_middle,
    turned_leaf, turned_middle, weights,
    edge_send, edge_recv, row_send, row_recv,
    pair_send, pair_recv, own, leaf_lines, middle_lines, final_send,
    coef_leaf, coef_middle,
    load_sem, factor_send_sem, factor_recv_sem, edge_send_sem, edge_recv_sem,
    row_send_sem, row_recv_sem,
    pair_send_sem, pair_recv_sem, right_send_sem, left_send_sem, right_recv_sem, left_recv_sem,
    final_send_sem, coef_leaf_sem, coef_middle_sem,
):
    front = lax.axis_index("dom")
    sep = lax.axis_index("sep")
    n_z = n_sep // 2
    z = sep // 2
    core = lax.rem(sep, 2)
    side = lax.rem(front, 2)
    group = lax.rem(front // 2, 2)
    across = flipped(front, 1)
    over = flipped(front, 2)
    sibling = flipped(sep, 1)
    beside = sep - 1 + 2 * core
    has_beside = jnp.logical_and(beside >= 0, beside < n_sep)
    n_beside = has_beside.astype(jnp.int32)
    not_first = (z > 0).astype(jnp.int32)
    not_last = (z < n_z - 1).astype(jnp.int32)

    rows, width = leaf_v.shape
    half = width // 2
    quarter = width // 4
    rank = couple_v.shape[2]
    own_rank = rank // 2
    n_top = quarter // CW
    n_mid = 2 * n_top
    n_leaf = 2 * n_mid

    loads = [
        pltpu.make_async_copy(front_rows_hbm, front_rows, load_sem.at[10]),
        pltpu.make_async_copy(rank_leaf_hbm, rank_leaf, load_sem.at[11]),
        pltpu.make_async_copy(rank_middle_hbm, rank_middle, load_sem.at[12]),
        pltpu.make_async_copy(pivot_leaf, pivot_v.at[0], load_sem.at[7]),
        pltpu.make_async_copy(pivot_middle.at[pl.ds(front // 2, 1)], pivot_v.at[1], load_sem.at[8]),
        pltpu.make_async_copy(pivot_top.at[pl.ds(front // 4, 1)], pivot_v.at[2], load_sem.at[9]),
        pltpu.make_async_copy(rhs_leaf.at[0], leaf_v, load_sem.at[0]),
        pltpu.make_async_copy(couple_leaf.at[0], couple_v.at[0], load_sem.at[1]),
        pltpu.make_async_copy(
            update_leaf.at[0], factor_leaf.at[side, pl.ds(0, rows)], load_sem.at[2]
        ),
        pltpu.make_async_copy(
            update_middle.at[0], factor_middle.at[group, pl.ds(0, rows)], load_sem.at[3]
        ),
        pltpu.make_async_copy(rhs_middle.at[0], middle_v, load_sem.at[4]),
        pltpu.make_async_copy(rhs_top.at[0], top_v, load_sem.at[5]),
        pltpu.make_async_copy(couple_middle.at[0], couple_v.at[1], load_sem.at[6]),
    ]
    for load in loads:
        load.start()

    barrier = pltpu.get_barrier_semaphore()

    def greet(dom_at, sep_at):
        pl.semaphore_signal(barrier, inc=1, device_id=(dom_at, sep_at), device_id_type=MESH)

    for dom_at in (front, across, over):
        greet(dom_at, sibling)
    for dom_at in (across, over):
        greet(dom_at, sep)

    @pl.when(has_beside)
    def _():
        for dom_at in (front, across, over):
            greet(dom_at, beside)

    @pl.when(z > 0)
    def _():
        greet(front, sep - 2)

    @pl.when(z < n_z - 1)
    def _():
        greet(front, sep + 2)

    @pl.when(sep == 0)
    def _():
        edge_recv[0] = jnp.zeros(edge_recv.shape[1:], F32)
        for slot in range(3):
            row_recv[slot, 0] = jnp.zeros(row_recv.shape[2:], F32)

    @pl.when(sep == n_sep - 1)
    def _():
        edge_recv[1] = jnp.zeros(edge_recv.shape[1:], F32)
        for slot in range(3):
            row_recv[slot, 1] = jnp.zeros(row_recv.shape[2:], F32)

    @pl.when(z == 0)
    def _():
        for lines in (leaf_lines, middle_lines):
            lines[2] = jnp.zeros(lines.shape[1:], lines.dtype)

    @pl.when(z == n_z - 1)
    def _():
        for lines in (leaf_lines, middle_lines):
            lines[3] = jnp.zeros(lines.shape[1:], lines.dtype)

    for load in loads[:6]:
        load.wait()
    row_at = lax.broadcasted_iota(jnp.int32, (rows, CW), 0)
    live = (row_at < front_rows[0, 0]).astype(F32)
    weights[0] = live * (1.0 / spread(pivot_v[0], CW))
    weights[1] = 1.0 / spread(pivot_v[1], CW)
    weights[2] = 1.0 / spread(pivot_v[2], CW)

    for load in loads[6:12]:
        load.wait()

    ends = (rows - 16, 0)
    picks = (15, 0)
    for way in range(2):
        block = pl.ds(ends[way], 16)
        pick = slice(picks[way], picks[way] + 1)
        leaf_row = leaf_v[block, :].astype(F32)[pick]
        leaf_weight = weights[0, block, :][pick][:, :1]
        edge_send[way, :, :width] = leaf_row * leaf_weight
        edge_send[way, :, width : width + half] = middle_v[block, :].astype(F32)[pick]
        edge_send[way, :, width + half : width + half + quarter] = (
            top_v[block, :].astype(F32)[pick]
        )
        tail = width + half + quarter
        edge_send[way, :, tail : tail + CW] = weights[1, block, :][pick]
        edge_send[way, :, tail + CW : tail + 2 * CW] = weights[2, block, :][pick]
        row_send[way, :, :rank] = factor_leaf[side, block, :].astype(F32)[pick]
        row_send[way, :, rank:] = factor_middle[group, block, :].astype(F32)[pick]

    pl.semaphore_wait(barrier, 5 + 3 * n_beside + not_first + not_last)

    def edge_copies(way, target):
        copies = [
            pltpu.make_async_remote_copy(
                edge_send.at[way], edge_recv.at[way], edge_send_sem.at[way],
                edge_recv_sem.at[way], device_id=(front, target), device_id_type=MESH,
            )
        ]
        for slot, dom_at in enumerate((front, across, over)):
            copies.append(
                pltpu.make_async_remote_copy(
                    row_send.at[way], row_recv.at[slot, way], row_send_sem.at[slot, way],
                    row_recv_sem.at[slot, way], device_id=(dom_at, target), device_id_type=MESH,
                )
            )
        return copies

    to_next = edge_copies(0, sep + 1)
    to_prev = edge_copies(1, sep - 1)

    @pl.when(sep < n_sep - 1)
    def _():
        for copy in to_next:
            copy.start()

    @pl.when(sep > 0)
    def _():
        for copy in to_prev:
            copy.start()

    factor_copies = [
        pltpu.make_async_remote_copy(
            factor_leaf.at[side, pl.ds(0, rows)], factor_leaf.at[side, pl.ds(0, rows)],
            factor_send_sem.at[0], factor_recv_sem.at[0],
            device_id=(across, sep), device_id_type=MESH,
        ),
        pltpu.make_async_remote_copy(
            factor_middle.at[group, pl.ds(0, rows)], factor_middle.at[group, pl.ds(0, rows)],
            factor_send_sem.at[1], factor_recv_sem.at[1],
            device_id=(over, sep), device_id_type=MESH,
        ),
    ]
    for copy in factor_copies:
        copy.start()

    def turn(which, turned):
        for part in range(2):
            at = pl.multiple_of(own_rank * (core if part == 0 else 1 - core), own_rank)
            turned[pl.ds(part * own_rank, own_rank), :] = couple_v[
                which, :, pl.ds(at, own_rank)
            ].T

    turn(0, turned_leaf)

    @pl.when(sep > 0)
    def _():
        to_next[0].wait_recv()

    @pl.when(sep < n_sep - 1)
    def _():
        to_prev[0].wait_recv()

    def solved(right_side, weight, before, after):
        scaled = right_side * weight
        up = jnp.where(row_at == 0, before, pltpu.roll(scaled, 1, 0))
        down = jnp.where(row_at == rows - 1, after, pltpu.roll(scaled, rows - 1, 0))
        return scaled + weight * (up + down)

    def place(i):
        here = lax.rem(i, 2)
        at_quarter = here * group + (1 - here) * (1 - group)
        return at_quarter * n_top + lax.div(i, 2)

    def to_device(src, dst, send_sem, recv_sem, dom_at, sep_at):
        return pltpu.make_async_remote_copy(
            src, dst, send_sem, recv_sem, device_id=(dom_at, sep_at), device_id_type=MESH
        )

    def pair_copy(slot):
        return to_device(
            pair_send.at[slot], pair_recv.at[slot], pair_send_sem.at[slot],
            pair_recv_sem.at[slot], front, sibling,
        )

    def right_copy(lines, first_slot, j):
        slot = first_slot + j
        return to_device(
            lines.at[0, j], lines.at[2, j], right_send_sem.at[slot],
            right_recv_sem.at[slot], front, sep + 2,
        )

    def left_copy(lines, first_slot, j):
        slot = first_slot + j
        return to_device(
            lines.at[1, j], lines.at[3, j], left_send_sem.at[slot],
            left_recv_sem.at[slot], front, sep - 2,
        )

    def final_copy(slot, coef, sem, child, i, dom_at, sep_at, lane):
        return to_device(
            final_send.at[slot],
            coef.at[child, i, pl.ds(pl.multiple_of(core * own_rank, own_rank), own_rank)],
            final_send_sem.at[slot, lax.rem(lane, 2)], sem.at[i, lane], dom_at, sep_at,
        )

    def start_pair(slot, turned, values):
        part = jnp.dot(turned[...], values, preferred_element_type=F32)
        own[slot] = part[:own_rank]
        pair_send[slot] = part[own_rank:]
        pair_copy(slot).start()

    def chain(t, count, base, first_slot, stride, lines, rank_now, coef, coef_sem, child, partner):
        def on(step, body):
            j = lax.div(step, stride) if stride > 1 else step
            hit = jnp.logical_and(step >= 0, step < stride * count)
            if stride > 1:
                hit = jnp.logical_and(hit, lax.rem(step, stride) == 0)

            @pl.when(hit)
            def _():
                body(j)

        def add_pair(j):
            slot = first_slot + j
            pair_copy(slot).wait_recv()
            own[slot] += pair_recv[slot]

        def prefix(j):
            slot = first_slot + j

            @pl.when(z > 0)
            def _():
                right_copy(lines, first_slot, j).wait_recv()

            @pl.when(z < n_z - 1)
            def _():
                lines[0, j] = (own[slot] + lines[2, j].astype(F32)).astype(lines.dtype)
                right_copy(lines, first_slot, j).start()

        def suffix(j):
            slot = first_slot + j

            @pl.when(z < n_z - 1)
            def _():
                left_copy(lines, first_slot, j).wait_recv()

            @pl.when(z > 0)
            def _():
                lines[1, j] = (own[slot] + lines[3, j].astype(F32)).astype(lines.dtype)
                left_copy(lines, first_slot, j).start()

        def final(j):
            slot = first_slot + j
            total = own[slot] + lines[2, j].astype(F32) + lines[3, j].astype(F32)
            at = core * own_rank + lax.broadcasted_iota(jnp.int32, total.shape, 0)
            kept = jnp.where(at < rank_now, total, 0.0).astype(BF16)
            final_send[slot] = kept
            i = lax.div(j, 2)

            @pl.when(lax.rem(j, 2) == 1)
            def _():
                coef[child, i, pl.ds(pl.multiple_of(core * own_rank, own_rank), own_rank)] = kept
                final_copy(slot, coef, coef_sem, child, i, front, sibling, 0).start()

            @pl.when(lax.rem(j, 2) == 0)
            def _():
                final_copy(slot, coef, coef_sem, child, i, partner, sep, 1).start()
                final_copy(slot, coef, coef_sem, child, i, partner, sibling, 2).start()

        start = t - base
        on(start, add_pair)
        on(start - z * HOP, prefix)
        on(start - (n_z - 1 - z) * HOP, suffix)
        on(start - jnp.maximum(z, n_z - 1 - z) * HOP, final)

    def await_coef(coef, sem, child, i):
        block = coef.at[child, i, pl.ds(0, own_rank)]
        for lane in range(3):
            to_device(
                final_send.at[0], block, final_send_sem.at[0, 0], sem.at[i, lane], front, sibling
            ).wait_recv()

    def applied(factor, coef, i):
        return jnp.dot(factor[0], coef[0, i], preferred_element_type=F32) + jnp.dot(
            factor[1], coef[1, i], preferred_element_type=F32
        )

    def leaf_step(j):
        i = lax.div(j, 2)
        own_side = lax.rem(j, 2)
        at_side = own_side * side + (1 - own_side) * (1 - side)
        at = pl.multiple_of(at_side * half + place(i) * CW, CW)
        values = solved(
            leaf_v[:, pl.ds(at, CW)].astype(F32), weights[0],
            edge_recv[0, :, pl.ds(at, CW)], edge_recv[1, :, pl.ds(at, CW)],
        ).astype(BF16)
        start_pair(j, turned_leaf, values)

    tail = width + half + quarter

    def eliminated(right_v, offset, at, factor, coef, i, which):
        taken = applied(factor, coef, i)
        beyond = []
        for way in range(2):
            right = edge_recv[way, :, pl.ds(pl.multiple_of(offset + at, CW), CW)]
            weight = edge_recv[way, :, tail + (which - 1) * CW : tail + which * CW]
            beyond.append((right - taken[rows + way : rows + way + 1]) * weight)
        return solved(
            right_v[:, pl.ds(at, CW)].astype(F32) - taken[:rows], weights[which], *beyond
        )

    def middle_step(i):
        await_coef(coef_leaf, coef_leaf_sem, side, i)
        at = pl.multiple_of(place(i) * CW, CW)
        values = eliminated(middle_v, width, at, factor_leaf, coef_leaf, i, 1).astype(BF16)
        start_pair(n_leaf + i, turned_middle, values)

    def top_step(i):
        await_coef(coef_middle, coef_middle_sem, group, i)
        at = pl.multiple_of(i * CW, CW)
        out[0, :, pl.ds(at, CW)] = eliminated(
            top_v, width + half, at, factor_middle, coef_middle, i, 2
        )

    def ready():
        loads[12].wait()
        turn(1, turned_middle)

        @pl.when(sep > 0)
        def _():
            for copy in to_next[1:]:
                copy.wait_recv()

        @pl.when(sep < n_sep - 1)
        def _():
            for copy in to_prev[1:]:
                copy.wait_recv()

        for copy in factor_copies:
            copy.wait_recv()

        at_row = lax.broadcasted_iota(jnp.int32, (16, rank), 0)

        def edge_tile(slot, lanes):
            before = row_recv[slot, 0, :, lanes]
            after = row_recv[slot, 1, :, lanes]
            tile = jnp.where(at_row == 0, before, jnp.where(at_row == 1, after, 0.0))
            return tile.astype(BF16)

        low, high = slice(0, rank), slice(rank, 2 * rank)
        factor_leaf[side, rows : rows + 16, :] = edge_tile(0, low)
        factor_leaf[1 - side, rows : rows + 16, :] = edge_tile(1, low)
        factor_middle[group, rows : rows + 16, :] = edge_tile(0, high)
        factor_middle[1 - group, rows : rows + 16, :] = edge_tile(2, high)

    leaf_base = LAG
    middle_at = leaf_base + (n_z - 1) * HOP + LAND + 1
    middle_base = middle_at + LAG
    top_at = middle_base + 2 + (n_z - 1) * HOP + LAND
    steps = top_at + 4 * (n_top - 1) + 1
    rank_leaf_now = rank_leaf[0]
    rank_middle_now = rank_middle[front // 2]

    def step(t, carry):
        @pl.when(t < n_leaf)
        def _():
            leaf_step(t)

        @pl.when(t == n_leaf)
        def _():
            ready()

        @pl.when(t < leaf_base + n_leaf + (n_z - 1) * HOP)
        def _():
            chain(
                t, n_leaf, leaf_base, 0, 1, leaf_lines, rank_leaf_now, coef_leaf, coef_leaf_sem,
                side, across,
            )

        i_mid = t - middle_at

        @pl.when(
            jnp.logical_and(i_mid >= 0, jnp.logical_and(i_mid < 2 * n_mid, lax.rem(i_mid, 2) == 0))
        )
        def _():
            middle_step(lax.div(i_mid, 2))

        @pl.when(t >= middle_base)
        def _():
            chain(
                t, n_mid, middle_base, n_leaf, 2, middle_lines, rank_middle_now, coef_middle,
                coef_middle_sem, group, over,
            )

        i_top = t - top_at

        @pl.when(jnp.logical_and(i_top >= 0, lax.rem(i_top, 4) == 0))
        def _():
            top_step(lax.div(i_top, 4))

        return carry

    lax.fori_loop(0, steps, step, 0)

    @pl.when(sep < n_sep - 1)
    def _():
        for copy in to_next:
            copy.wait_send()

    @pl.when(sep > 0)
    def _():
        for copy in to_prev:
            copy.wait_send()

    for copy in factor_copies:
        copy.wait_send()

    def drain(lines, first_slot, j, carry):
        slot = first_slot + j
        pair_copy(slot).wait_send()

        @pl.when(z < n_z - 1)
        def _():
            right_copy(lines, first_slot, j).wait_send()

        @pl.when(z > 0)
        def _():
            left_copy(lines, first_slot, j).wait_send()

        final_copy(slot, coef_leaf, coef_leaf_sem, side, 0, front, sibling, 0).wait_send()

        @pl.when(lax.rem(j, 2) == 0)
        def _():
            final_copy(slot, coef_leaf, coef_leaf_sem, side, 0, across, sep, 1).wait_send()

        return carry

    lax.fori_loop(0, n_leaf, functools.partial(drain, leaf_lines, 0), 0)
    lax.fori_loop(0, n_mid, functools.partial(drain, middle_lines, n_leaf), 0)


def shards(*operands):
    n_sep = lax.axis_size("sep")
    rows, width = operands[0].shape[1:]
    rank = operands[3].shape[2]
    half, quarter = width // 2, width // 4
    own_rank = rank // 2
    n_top = quarter // CW
    n_mid = 2 * n_top
    slots = 3 * n_mid
    chunk = (slots, own_rank, CW)
    tail = width + half + quarter + 2 * CW
    dma = pltpu.SemaphoreType.DMA
    hbm = pl.BlockSpec(memory_space=pltpu.HBM)
    vmem = pl.BlockSpec(memory_space=pltpu.VMEM)
    return pl.pallas_call(
        functools.partial(kernel, n_sep),
        out_shape=jax.ShapeDtypeStruct((1, rows, quarter), F32),
        in_specs=[hbm] * 13,
        out_specs=vmem,
        scratch_shapes=[
            pltpu.SMEM(operands[10].shape, jnp.int32),
            pltpu.SMEM(operands[11].shape, jnp.int32),
            pltpu.SMEM(operands[12].shape, jnp.int32),
            pltpu.VMEM((3, 1, rows), F32),
            pltpu.VMEM((rows, width), BF16),
            pltpu.VMEM((rows, half), BF16),
            pltpu.VMEM((rows, quarter), BF16),
            pltpu.VMEM((2, rows, rank), BF16),
            pltpu.VMEM((2, rows + 16, rank), BF16),
            pltpu.VMEM((2, rows + 16, rank), BF16),
            pltpu.VMEM((rank, rows), BF16),
            pltpu.VMEM((rank, rows), BF16),
            pltpu.VMEM((3, rows, CW), F32),
            pltpu.VMEM((2, 1, tail), F32),
            pltpu.VMEM((2, 1, tail), F32),
            pltpu.VMEM((2, 1, 2 * rank), F32),
            pltpu.VMEM((3, 2, 1, 2 * rank), F32),
            pltpu.VMEM(chunk, F32),
            pltpu.VMEM(chunk, F32),
            pltpu.VMEM(chunk, F32),
            pltpu.VMEM((4, 2 * n_mid, own_rank, CW), BF16),
            pltpu.VMEM((4, n_mid, own_rank, CW), F32),
            pltpu.VMEM(chunk, BF16),
            pltpu.VMEM((2, n_mid, rank, CW), BF16),
            pltpu.VMEM((2, n_top, rank, CW), BF16),
            dma((13,)),
            dma((2,)),
            dma((2,)),
            dma((2,)),
            dma((2,)),
            dma((3, 2)),
            dma((3, 2)),
            dma((slots,)),
            dma((slots,)),
            dma((slots,)),
            dma((slots,)),
            dma((slots,)),
            dma((slots,)),
            dma((slots, 2)),
            dma((n_mid, 3)),
            dma((n_top, 3)),
        ],
        compiler_params=pltpu.CompilerParams(
            collective_id=0, has_side_effects=True, vmem_limit_bytes=67043328
        ),
    )(*operands)


def solution(mesh):
    return jax.shard_map(
        shards,
        mesh=mesh,
        in_specs=(
            P("dom", "sep", None),
            P("dom", "sep", None),
            P("dom", "sep", None),
            P("dom", "sep", None),
            P("dom", "sep", None),
            P("dom", "sep", None),
            P("dom", "sep", None),
            P("dom", "sep"),
            P(None, "sep"),
            P(None, "sep"),
            P("dom", "sep"),
            P("dom"),
            P(),
        ),
        out_specs=P("dom", "sep", None),
        check_vma=False,
    )
```

profile of v0, /device:TPU:0, one launch (start us, length us, event | category | flops | bytes accessed | tf_op | source)
XLA Modules:
  0.0 50.7 jit_solution(1826644355205197867)
XLA Ops:
  1.3 47.3 %shard_map.127 = f32[1,512,384]{2,1,0:T(8,128)} custom-call(bf16[1,512,1536]{2,1,0:T(8,128)(2,1)} %rhs_leaf.1, bf16[1,512,768]{2,1,0:T(8,128)(2,1)} %rhs_middle.1, bf16[1,512,384]{2,1,0:T(8,128)(2,1)} %rhs_top.1, bf16[1,512,256]{2,1,0:T(8,128)(2,1)} %update_leaf.1, bf16[1,512,256]{2,1,0:T(8,128)(2,1)} %couple_leaf.1, bf16[1,512,256]{2,1,0:T(8,128)(2,1)} %update_middle.1, ...), custom_call_target="tpu_custom_call" | custom-call | tf_op jit(solution)/shard_map/pallas_call | solution.py:520
  48.6 2.1 %copy.17 = f32[1,512,384]{2,1,0:T(8,128)} copy(f32[1,512,384]{2,1,0:T(8,128)} %shard_map.127) | data formatting | bytes 1572864
where the time goes:
time: 50.9 us; the launch traced here: 50.7 us
  Pallas kernels  47.3 us (93%)
  local copies, waits for them, and re-layouts  2.06 us (4%)
  between operations  1.3 us (3%)
    pallas_call x1, Pallas kernels, shards(): pl.pallas_call(functools.partial(kernel, n_sep), out_shape=jax.ShapeDtype...  47.3 us
    unnamed x1, local copies, waits for them, and re-layouts  2.06 us

commit v1 on v0

v1 whole, which is shorter than its diff:
```python
import functools

import jax
import jax.numpy as jnp
from jax import lax
from jax.experimental import pallas as pl
from jax.experimental.pallas import tpu as pltpu
from jax.sharding import PartitionSpec as P

MESH = pl.DeviceIdType.MESH
F32 = jnp.float32
BF16 = jnp.bfloat16
CW = 128
HOP = 5
LAND = 2
TILE = 16


def flipped(value, bit):
    return value + bit - 2 * bit * (lax.rem(value // bit, 2))


def spread(row, height):
    return jnp.broadcast_to(row, (height, row.shape[1])).T


def dot(a, b):
    return jnp.dot(a, b, preferred_element_type=F32)


def dot_rows(a, b):
    return lax.dot_general(a, b, (((0,), (0,)), ((), ())), preferred_element_type=F32)


def kernel(
    n_sep,
    rhs_leaf, rhs_middle, rhs_top, update_leaf, couple_leaf, update_middle, couple_middle,
    pivot_leaf, pivot_middle, pivot_top, front_rows_hbm, rank_leaf_hbm, rank_middle_hbm,
    out,
    front_rows, rank_leaf, rank_middle, pivot_v, pivot_edge,
    leaf_v, middle_v, top_v, top_edge, couple_l, couple_m, update_l, update_m,
    weights, turned_l, turned_high, turned_low,
    edges, edge_left, edge_right, pair_g_send, pair_g_recv, g_own, g_send, g_recv, g_twice,
    coef_l, m_own, m_send, m_recv, p_send, p_recv, own,
    right_send, right_recv, left_send, left_recv, coef_m,
    load_sem, edge_send_sem, edge_recv_sem, tile_send_sem, tile_recv_sem,
    factor_send_sem, factor_recv_sem, pair_send_sem, pair_recv_sem, g_send_sem, g_recv_sem,
    coef_send_sem, coef_recv_sem, p_send_sem, p_recv_sem,
    right_send_sem, right_recv_sem, left_send_sem, left_recv_sem,
    final_send_sem, final_recv_sem,
):
    front = lax.axis_index("dom")
    sep = lax.axis_index("sep")
    n_z = n_sep // 2
    z = sep // 2
    core = lax.rem(sep, 2)
    side = lax.rem(front, 2)
    group = lax.rem(front // 2, 2)
    across = flipped(front, 1)
    over = flipped(front, 2)
    beyond = flipped(across, 2)
    sibling = flipped(sep, 1)

    rows, width = leaf_v.shape
    half = width // 2
    quarter = width // 4
    rank = couple_l.shape[1]
    hr = rank // 2
    n_top = quarter // CW
    items = 2 * n_top

    def load(src, dst, slot):
        return pltpu.make_async_copy(src, dst, load_sem.at[slot])

    loads = [
        load(front_rows_hbm, front_rows, 0),
        load(rank_leaf_hbm, rank_leaf, 1),
        load(rank_middle_hbm, rank_middle, 2),
        load(pivot_middle.at[pl.ds(front // 2, 1)], pivot_v.at[1], 3),
        load(couple_middle.at[0], couple_m, 4),
        load(update_leaf.at[0], update_l, 5),
        load(pivot_leaf, pivot_v.at[0], 6),
        load(couple_leaf.at[0], couple_l, 7),
        load(pivot_top.at[pl.ds(front // 4, 1)], pivot_v.at[2], 8),
        load(update_middle.at[0], update_m.at[group, pl.ds(0, rows)], 9),
        load(rhs_top.at[0], top_v, 10),
        load(rhs_leaf.at[0], leaf_v, 11),
        load(rhs_middle.at[0], middle_v, 12),
    ]
    for one in loads:
        one.start()

    barrier = pltpu.get_barrier_semaphore()

    def greet(dom_at, sep_at):
        pl.semaphore_signal(barrier, inc=1, device_id=(dom_at, sep_at), device_id_type=MESH)

    for k in range(1, n_sep):
        greet(front, lax.rem(sep + k, n_sep))
    for dom_at in (across, over, beyond):
        greet(dom_at, sep)
    has_prev = (sep > 0).astype(jnp.int32)
    has_next = (sep < n_sep - 1).astype(jnp.int32)

    @pl.when(sep > 0)
    def _():
        greet(over, sep - 1)

    @pl.when(sep < n_sep - 1)
    def _():
        greet(over, sep + 1)

    def clear(way):
        pivot_edge[way] = jnp.ones(pivot_edge.shape[1:], F32)
        top_edge[way] = jnp.zeros(top_edge.shape[1:], BF16)
        for g in range(2):
            update_m[g, rows + way * TILE : rows + (way + 1) * TILE, :] = jnp.zeros(
                (TILE, rank), BF16
            )

    @pl.when(sep == 0)
    def _():
        clear(0)

    @pl.when(sep == n_sep - 1)
    def _():
        clear(1)

    @pl.when(z == 0)
    def _():
        right_recv[...] = jnp.zeros(right_recv.shape, BF16)

    @pl.when(z == n_z - 1)
    def _():
        left_recv[...] = jnp.zeros(left_recv.shape, BF16)

    row_at = lax.broadcasted_iota(jnp.int32, (rows, CW), 0)
    lane_at = lax.broadcasted_iota(jnp.int32, (rows, CW), 1)

    def shifted(scaled, before, after):
        up = jnp.where(row_at == 0, before, pltpu.roll(scaled, 1, 0))
        down = jnp.where(row_at == rows - 1, after, pltpu.roll(scaled, rows - 1, 0))
        return up + down

    def half_at(which):
        return pl.multiple_of(hr * which, hr)

    def weighed(couple, which, weight, rank_now):
        at = half_at(which)
        kept = jnp.where(lane_at + at < rank_now, couple[:, pl.ds(at, hr)].astype(F32), 0.0)
        scaled = kept * weight
        return scaled, scaled + weight * shifted(scaled, 0.0, 0.0)

    def note(column, which, scaled):
        at = half_at(which)
        for end, edge_row in ((0, rows - 1), (1, 0)):
            edges[sep, :, pl.ds((column + end) * rank + at, hr)] = scaled[edge_row : edge_row + 1]

    rank_leaf_now = None
    for one in loads[:5]:
        one.wait()
    rank_leaf_now = rank_leaf[0]
    rank_middle_now = rank_middle[front // 2]
    weights[1] = 1.0 / spread(pivot_v[1], CW)
    for part, which in ((1, 1 - core), (0, core)):
        scaled, full = weighed(couple_m, which, weights[1], rank_middle_now)
        note(0, which, scaled)
        turned = full.T
        high = turned.astype(BF16)
        turned_high[part * hr : (part + 1) * hr, :] = high
        turned_low[part * hr : (part + 1) * hr, :] = (turned - high.astype(F32)).astype(BF16)

    loads[5].wait()

    def by_middle(part, right):
        block = slice(part * hr, (part + 1) * hr)
        return dot(turned_high[block, :], right) + dot(turned_low[block, :], right)

    pair_g_send[...] = by_middle(1, update_l[...])

    pl.semaphore_wait(barrier, n_sep + 2 + has_prev + has_next)

    def to_device(src, dst, send_sem, recv_sem, dom_at, sep_at):
        return pltpu.make_async_remote_copy(
            src, dst, send_sem, recv_sem, device_id=(dom_at, sep_at), device_id_type=MESH
        )

    pair_g = to_device(
        pair_g_send, pair_g_recv, pair_send_sem.at[0], pair_recv_sem.at[0], front, sibling
    )
    pair_g.start()
    g_own[...] = by_middle(0, update_l[...])

    for end, edge_row in ((0, rows - 1), (1, 0)):
        block = pl.ds(rows - TILE if end == 0 else 0, TILE)
        pick = TILE - 1 if end == 0 else 0
        row = update_l[block, :].astype(F32)[pick : pick + 1]
        edges[sep, :, (2 + end) * rank : (3 + end) * rank] = (
            row * weights[1, block, :][pick : pick + 1, :1]
        )

    for one in loads[6:8]:
        one.wait()
    live = (row_at < front_rows[0, 0]).astype(F32)
    weights[0] = live * (1.0 / spread(pivot_v[0], CW))
    for which in range(2):
        scaled, full = weighed(couple_l, which, weights[0], rank_leaf_now)
        note(4, which, scaled)
        turned_l[which * hr : (which + 1) * hr, :] = full.astype(BF16).T

    def edge_copy(sep_at, source):
        return to_device(
            edges.at[source], edges.at[source], edge_send_sem.at[sep_at],
            edge_recv_sem.at[source], front, sep_at,
        )

    pair_g.wait_recv()
    summed = g_own[...] + pair_g_recv[...]
    g_own[...] = summed
    g_send[...] = summed.astype(BF16)

    def g_copy(z_at, source):
        return to_device(
            g_send, g_recv.at[source], g_send_sem.at[z_at], g_recv_sem.at[source],
            front, 2 * z_at + core,
        )

    for k in range(1, n_sep):
        edge_copy(lax.rem(sep + k, n_sep), sep).start()
    for k in range(1, n_z):
        g_copy(lax.rem(z + k, n_z), z).start()

    for one in loads[8:11]:
        one.wait()

    def tile_copies(way, sep_at):
        block = pl.ds(rows - TILE if way == 0 else 0, TILE)
        landing = pl.ds(rows + way * TILE, TILE)
        copies = [
            (pivot_v.at[2], pivot_edge.at[way], front),
            (top_v.at[block], top_edge.at[way], front),
            (update_m.at[group, block], update_m.at[group, landing], front),
            (update_m.at[group, block], update_m.at[group, landing], over),
        ]
        return [
            to_device(
                src, dst, tile_send_sem.at[way, n], tile_recv_sem.at[way, n], dom_at, sep_at
            )
            for n, (src, dst, dom_at) in enumerate(copies)
        ]

    to_next = tile_copies(0, sep + 1)
    to_prev = tile_copies(1, sep - 1)

    @pl.when(sep < n_sep - 1)
    def _():
        for copy in to_next:
            copy.start()

    @pl.when(sep > 0)
    def _():
        for copy in to_prev:
            copy.start()

    factor_copy = to_device(
        update_m.at[group, pl.ds(0, rows)], update_m.at[group, pl.ds(0, rows)],
        factor_send_sem.at[0], factor_recv_sem.at[0], over, sep,
    )
    factor_copy.start()
    weights[2] = 1.0 / spread(pivot_v[2], CW)

    for one in loads[11:]:
        one.wait()
    for k in range(1, n_sep):
        edge_copy(0, lax.rem(sep + k, n_sep)).wait_recv()

    sixteen = lax.broadcasted_iota(jnp.int32, (TILE, rank), 0)
    before_at = jnp.maximum(sep - 1, 0)
    after_at = jnp.minimum(sep + 1, n_sep - 1)

    def two_rows(height_at, first, second):
        return jnp.where(height_at == 0, first, jnp.where(height_at == 1, second, 0.0)).astype(BF16)

    def neighbours(column):
        before = edges[before_at, :, column * rank : (column + 1) * rank]
        after = edges[after_at, :, (column + 1) * rank : (column + 2) * rank]
        return two_rows(
            sixteen, jnp.where(sep > 0, before, 0.0), jnp.where(sep < n_sep - 1, after, 0.0)
        )

    def end_rows(right, which, columns):
        first = right[0:TILE, columns].astype(F32)[0:1] * weights[which, 0:TILE, :][0:1, :1]
        last = (
            right[rows - TILE : rows, columns].astype(F32)[TILE - 1 :]
            * weights[which, rows - TILE : rows, :][TILE - 1 :, :1]
        )
        return two_rows(
            lax.broadcasted_iota(jnp.int32, (TILE, first.shape[1]), 0), first, last
        )

    edge_left[...] = neighbours(4)

    def coef_copy(n):
        columns = pl.ds(n * quarter, quarter)
        return to_device(
            coef_l.at[pl.ds(0, rank), columns], coef_l.at[pl.ds(rank, rank), columns],
            coef_send_sem.at[n], coef_recv_sem.at[n], front, sibling,
        )

    for n in range(4):
        columns = slice(n * quarter, (n + 1) * quarter)
        coef_l[0:rank, columns] = (
            dot(turned_l[...], leaf_v[:, columns])
            + dot_rows(edge_left[...], end_rows(leaf_v, 0, columns))
        ).astype(BF16)
        coef_copy(n).start()

    edge_left[...] = neighbours(0)
    m_pair = to_device(m_send, m_recv, pair_send_sem.at[1], pair_recv_sem.at[1], front, sibling)
    for part, which, target in ((1, 1 - core, m_send), (0, core, m_own)):
        for n in range(2):
            columns = slice(n * quarter, (n + 1) * quarter)
            target[:, columns] = by_middle(part, middle_v[:, columns]) + dot_rows(
                edge_left[:, pl.ds(half_at(which), hr)], end_rows(middle_v, 1, columns)
            )
        if part == 1:
            m_pair.start()

    own_lanes = half_at(core)
    for b in range(n_sep):
        if b < n_sep - 1:
            left = (
                edges[b, :, pl.ds(own_lanes, hr)], edges[b + 1, :, pl.ds(rank + own_lanes, hr)],
            )
            right = (
                edges[b + 1, :, 3 * rank : 4 * rank], edges[b, :, 2 * rank : 3 * rank],
            )
        else:
            left = (jnp.zeros((1, hr), F32),) * 2
            right = (jnp.zeros((1, rank), F32),) * 2
        for n in range(2):
            edge_right[2 * b + n : 2 * b + n + 1, :rank] = right[n]
            edge_right[2 * b + n : 2 * b + n + 1, rank:] = left[n]
    total = g_own[...] + dot_rows(
        edge_right[:, rank:].astype(BF16), edge_right[:, :rank].astype(BF16)
    )
    m_pair.wait_recv()
    m_own[...] += m_recv[...]
    for n in range(4):
        coef_copy(n).wait_recv()
    g_own[...] = total
    for k in range(1, n_z):
        source = lax.rem(z + k, n_z)
        g_copy(0, source).wait_recv()
        g_own[...] += g_recv[source].astype(F32)
    negated = (-g_own[...]).astype(BF16)
    g_twice[:, :rank] = negated
    g_twice[:, rank:] = negated

    targets = (across, over, beyond)

    def p_copy(n, j):
        return to_device(
            p_send.at[n, j], p_recv.at[n, j], p_send_sem.at[n, j], p_recv_sem.at[n, j],
            targets[n], sep,
        )

    def piece(side_at, group_at, j):
        at = pl.multiple_of(side_at * half + group_at * quarter + j * CW, CW)
        return dot(g_twice[...], coef_l[:, pl.ds(at, CW)])

    def m_piece(group_at, j):
        return m_own[:, pl.ds(pl.multiple_of(group_at * quarter + j * CW, CW), CW)]

    for j in range(n_top):
        p_send[2, j] = piece(1 - side, 1 - group, j).astype(BF16)
        p_copy(2, j).start()
        p_send[1, j] = (piece(side, 1 - group, j) + m_piece(1 - group, j)).astype(BF16)
        p_copy(1, j).start()
        p_send[0, j] = piece(1 - side, group, j).astype(BF16)
        p_copy(0, j).start()
        own[2 * j] = piece(side, group, j) + m_piece(group, j)

    @pl.when(sep > 0)
    def _():
        for copy in to_next:
            copy.wait_recv()

    @pl.when(sep < n_sep - 1)
    def _():
        for copy in to_prev:
            copy.wait_recv()

    factor_copy.wait_recv()

    def right_copy(i):
        return to_device(
            right_send.at[i], right_recv.at[i], right_send_sem.at[i], right_recv_sem.at[i],
            front, sep + 2,
        )

    def left_copy(i):
        return to_device(
            left_send.at[i], left_recv.at[i], left_send_sem.at[i], left_recv_sem.at[i],
            front, sep - 2,
        )

    def final_copy(i):
        at = lax.rem(i, 2)
        place = coef_m.at[
            group + at - 2 * group * at, lax.div(i, 2), :, pl.ds(half_at(core), hr)
        ]
        return to_device(
            place, place, final_send_sem.at[i], final_recv_sem.at[i], front, sibling
        )

    def gather(i):
        j = lax.div(i, 2)

        @pl.when(lax.rem(i, 2) == 0)
        def _():
            p_copy(0, j).wait_recv()
            own[i] += p_recv[0, j].astype(F32)

        @pl.when(lax.rem(i, 2) == 1)
        def _():
            p_copy(1, j).wait_recv()
            p_copy(2, j).wait_recv()
            own[i] = p_recv[1, j].astype(F32) + p_recv[2, j].astype(F32)

    def prefix(i):
        @pl.when(z > 0)
        def _():
            right_copy(i).wait_recv()

        @pl.when(z < n_z - 1)
        def _():
            right_send[i] = (own[i] + right_recv[i].astype(F32)).astype(BF16)
            right_copy(i).start()

    def suffix(i):
        @pl.when(z < n_z - 1)
        def _():
            left_copy(i).wait_recv()

        @pl.when(z > 0)
        def _():
            left_send[i] = (own[i] + left_recv[i].astype(F32)).astype(BF16)
            left_copy(i).start()

    def final(i):
        total = own[i] + right_recv[i].astype(F32) + left_recv[i].astype(F32)
        high = total.astype(BF16)
        low = (total - high.astype(F32)).astype(BF16)
        at = lax.rem(i, 2)
        group_at = group + at - 2 * group * at
        coef_m[group_at, lax.div(i, 2), 0, pl.ds(half_at(core), hr)] = high
        coef_m[group_at, lax.div(i, 2), 1, pl.ds(half_at(core), hr)] = low
        final_copy(i).start()

    def top(j):
        final_copy(2 * j).wait_recv()
        final_copy(2 * j + 1).wait_recv()
        at = pl.multiple_of(j * CW, CW)
        taken = (
            dot(update_m[0], coef_m[0, j, 0]) + dot(update_m[1], coef_m[1, j, 0])
            + dot(update_m[0], coef_m[0, j, 1]) + dot(update_m[1], coef_m[1, j, 1])
        )
        before = (
            top_edge[0, :, pl.ds(at, CW)].astype(F32)[TILE - 1 :]
            - taken[rows + TILE - 1 : rows + TILE]
        ) / pivot_edge[0, :, rows - 1 :]
        after = (
            top_edge[1, :, pl.ds(at, CW)].astype(F32)[:1] - taken[rows + TILE : rows + TILE + 1]
        ) / pivot_edge[1, :, :1]
        scaled = (top_v[:, pl.ds(at, CW)].astype(F32) - taken[:rows]) * weights[2]
        out[0, :, pl.ds(at, CW)] = scaled + weights[2] * shifted(scaled, before, after)

    last = jnp.maximum(z, n_z - 1 - z) * HOP
    steps = (n_z - 1) * HOP + items + LAND

    def step(t, carry):
        def on(at, count, body):
            @pl.when(jnp.logical_and(at >= 0, at < count))
            def _():
                body(at)

        on(t, items, gather)
        on(t - z * HOP, items, prefix)
        on(t - (n_z - 1 - z) * HOP, items, suffix)
        on(t - last, items, final)
        done = t - last - 1 - LAND

        @pl.when(jnp.logical_and(done >= 0, jnp.logical_and(done < items, lax.rem(done, 2) == 0)))
        def _():
            top(lax.div(done, 2))

        return carry

    lax.fori_loop(0, steps, step, 0)

    pair_g.wait_send()
    m_pair.wait_send()
    factor_copy.wait_send()
    for k in range(1, n_sep):
        edge_copy(lax.rem(sep + k, n_sep), sep).wait_send()
    for k in range(1, n_z):
        g_copy(lax.rem(z + k, n_z), z).wait_send()
    for n in range(4):
        coef_copy(n).wait_send()
    for n in range(3):
        for j in range(n_top):
            p_copy(n, j).wait_send()

    @pl.when(sep < n_sep - 1)
    def _():
        for copy in to_next:
            copy.wait_send()

    @pl.when(sep > 0)
    def _():
        for copy in to_prev:
            copy.wait_send()

    def drain(i, carry):
        @pl.when(z < n_z - 1)
        def _():
            right_copy(i).wait_send()

        @pl.when(z > 0)
        def _():
            left_copy(i).wait_send()

        final_copy(i).wait_send()
        return carry

    lax.fori_loop(0, items, drain, 0)


def shards(*operands):
    n_sep = lax.axis_size("sep")
    rows, width = operands[0].shape[1:]
    rank = operands[3].shape[2]
    half, quarter = width // 2, width // 4
    hr = rank // 2
    n_top = quarter // CW
    items = 2 * n_top
    dma = pltpu.SemaphoreType.DMA
    hbm = pl.BlockSpec(memory_space=pltpu.HBM)
    vmem = pl.BlockSpec(memory_space=pltpu.VMEM)
    return pl.pallas_call(
        functools.partial(kernel, n_sep),
        out_shape=jax.ShapeDtypeStruct((1, rows, quarter), F32),
        in_specs=[hbm] * 13,
        out_specs=vmem,
        scratch_shapes=[
            pltpu.SMEM(operands[10].shape, jnp.int32),
            pltpu.SMEM(operands[11].shape, jnp.int32),
            pltpu.SMEM(operands[12].shape, jnp.int32),
            pltpu.VMEM((3, 1, rows), F32),
            pltpu.VMEM((2, 1, rows), F32),
            pltpu.VMEM((rows, width), BF16),
            pltpu.VMEM((rows, half), BF16),
            pltpu.VMEM((rows, quarter), BF16),
            pltpu.VMEM((2, TILE, quarter), BF16),
            pltpu.VMEM((rows, rank), BF16),
            pltpu.VMEM((rows, rank), BF16),
            pltpu.VMEM((rows, rank), BF16),
            pltpu.VMEM((2, rows + 2 * TILE, rank), BF16),
            pltpu.VMEM((3, rows, CW), F32),
            pltpu.VMEM((rank, rows), BF16),
            pltpu.VMEM((rank, rows), BF16),
            pltpu.VMEM((rank, rows), BF16),
            pltpu.VMEM((n_sep, 1, 6 * rank), F32),
            pltpu.VMEM((TILE, rank), BF16),
            pltpu.VMEM((2 * n_sep, rank + hr), F32),
            pltpu.VMEM((hr, rank), F32),
            pltpu.VMEM((hr, rank), F32),
            pltpu.VMEM((hr, rank), F32),
            pltpu.VMEM((hr, rank), BF16),
            pltpu.VMEM((n_sep // 2, hr, rank), BF16),
            pltpu.VMEM((hr, 2 * rank), BF16),
            pltpu.VMEM((2 * rank, width), BF16),
            pltpu.VMEM((hr, half), F32),
            pltpu.VMEM((hr, half), F32),
            pltpu.VMEM((hr, half), F32),
            pltpu.VMEM((3, n_top, hr, CW), BF16),
            pltpu.VMEM((3, n_top, hr, CW), BF16),
            pltpu.VMEM((items, hr, CW), F32),
            pltpu.VMEM((items, hr, CW), BF16),
            pltpu.VMEM((items, hr, CW), BF16),
            pltpu.VMEM((items, hr, CW), BF16),
            pltpu.VMEM((items, hr, CW), BF16),
            pltpu.VMEM((2, n_top, 2, rank, CW), BF16),
            dma((13,)),
            dma((n_sep,)),
            dma((n_sep,)),
            dma((2, 4)),
            dma((2, 4)),
            dma((1,)),
            dma((1,)),
            dma((2,)),
            dma((2,)),
            dma((n_sep // 2,)),
            dma((n_sep // 2,)),
            dma((4,)),
            dma((4,)),
            dma((3, n_top)),
            dma((3, n_top)),
            dma((items,)),
            dma((items,)),
            dma((items,)),
            dma((items,)),
            dma((items,)),
            dma((items,)),
        ],
        compiler_params=pltpu.CompilerParams(
            collective_id=0, has_side_effects=True, vmem_limit_bytes=67043328
        ),
    )(*operands)


def solution(mesh):
    return jax.shard_map(
        shards,
        mesh=mesh,
        in_specs=(
            P("dom", "sep", None),
            P("dom", "sep", None),
            P("dom", "sep", None),
            P("dom", "sep", None),
            P("dom", "sep", None),
            P("dom", "sep", None),
            P("dom", "sep", None),
            P("dom", "sep"),
            P(None, "sep"),
            P(None, "sep"),
            P("dom", "sep"),
            P("dom"),
            P(),
        ),
        out_specs=P("dom", "sep", None),
        check_vma=False,
    )
```

time: 50.9 us -> 39.3 us (0.77)
  Pallas kernels: 47.3 us -> 35.5 us
    pallas_call x1, Pallas kernels: 47.3 us -> 35.5 us  [shards(): pl.pallas_call(functools.partial(kernel, n_sep), out_shape=jax.ShapeDtype...]
where the time goes in v1:
time: 39.3 us; the launch traced here: 38.9 us
  Pallas kernels  35.5 us (90%)
  local copies, waits for them, and re-layouts  2.06 us (5%)
  between operations  1.3 us (3%)
    pallas_call x1, Pallas kernels, shards(): pl.pallas_call(functools.partial(kernel, n_sep), out_shape=jax.ShapeDtype...  35.5 us
    unnamed x1, local copies, waits for them, and re-layouts  2.06 us

profile of v1, /device:TPU:0, one launch (start us, length us, event | category | flops | bytes accessed | tf_op | source)
XLA Modules:
  0.0 38.9 jit_solution(2730580754587806522)
XLA Ops:
  1.3 35.5 %shard_map.127 = f32[1,512,384]{2,1,0:T(8,128)} custom-call(bf16[1,512,1536]{2,1,0:T(8,128)(2,1)} %rhs_leaf.1, bf16[1,512,768]{2,1,0:T(8,128)(2,1)} %rhs_middle.1, bf16[1,512,384]{2,1,0:T(8,128)(2,1)} %rhs_top.1, bf16[1,512,256]{2,1,0:T(8,128)(2,1)} %update_leaf.1, bf16[1,512,256]{2,1,0:T(8,128)(2,1)} %couple_leaf.1, bf16[1,512,256]{2,1,0:T(8,128)(2,1)} %update_middle.1, ...), custom_call_target="tpu_custom_call" | custom-call | tf_op jit(solution)/shard_map/pallas_call | solution.py:551
  36.9 2.1 %copy.17 = f32[1,512,384]{2,1,0:T(8,128)} copy(f32[1,512,384]{2,1,0:T(8,128)} %shard_map.127) | data formatting | bytes 1572864

commit v2 on v1

--- a/solution.py
+++ b/solution.py
@@ -11,8 +11,9 @@
 F32 = jnp.float32
 BF16 = jnp.bfloat16
 CW = 128
-HOP = 5
-LAND = 2
+PARTS = 2
+HOP = 5 * PARTS
+LAND = 2 * PARTS
 TILE = 16
 
 
@@ -67,7 +68,9 @@
     rank = couple_l.shape[1]
     hr = rank // 2
     n_top = quarter // CW
-    items = 2 * n_top
+    hp = hr // PARTS
+    pieces = 2 * n_top
+    items = PARTS * pieces
 
     def load(src, dst, slot):
         return pltpu.make_async_copy(src, dst, load_sem.at[slot])
@@ -151,10 +154,10 @@
         scaled = kept * weight
         return scaled, scaled + weight * shifted(scaled, 0.0, 0.0)
 
-    def note(column, which, scaled):
-        at = half_at(which)
+    def note(at, stride, scaled):
         for end, edge_row in ((0, rows - 1), (1, 0)):
-            edges[sep, :, pl.ds((column + end) * rank + at, hr)] = scaled[edge_row : edge_row + 1]
+            place = pl.multiple_of(at + end * stride, hr)
+            edges[sep, :, pl.ds(place, hr)] = scaled[edge_row : edge_row + 1]
 
     rank_leaf_now = None
     for one in loads[:5]:
@@ -164,7 +167,7 @@
     weights[1] = 1.0 / spread(pivot_v[1], CW)
     for part, which in ((1, 1 - core), (0, core)):
         scaled, full = weighed(couple_m, which, weights[1], rank_middle_now)
-        note(0, which, scaled)
+        note(which * 6 * hr, hr, scaled)
         turned = full.T
         high = turned.astype(BF16)
         turned_high[part * hr : (part + 1) * hr, :] = high
@@ -195,7 +198,7 @@
         block = pl.ds(rows - TILE if end == 0 else 0, TILE)
         pick = TILE - 1 if end == 0 else 0
         row = update_l[block, :].astype(F32)[pick : pick + 1]
-        edges[sep, :, (2 + end) * rank : (3 + end) * rank] = (
+        edges[sep, :, (1 + end) * rank : (2 + end) * rank] = (
             row * weights[1, block, :][pick : pick + 1, :1]
         )
 
@@ -205,30 +208,47 @@
     weights[0] = live * (1.0 / spread(pivot_v[0], CW))
     for which in range(2):
         scaled, full = weighed(couple_l, which, weights[0], rank_leaf_now)
-        note(4, which, scaled)
+        note((8 + which) * hr, rank, scaled)
         turned_l[which * hr : (which + 1) * hr, :] = full.astype(BF16).T
 
-    def edge_copy(sep_at, source):
+    def edge_copy(k, sep_at, source, core_at):
+        place = edges.at[source]
+        if k not in (1, n_sep - 1):
+            place = edges.at[source, :, pl.ds(pl.multiple_of(rank * core_at, rank), 6 * hr)]
         return to_device(
-            edges.at[source], edges.at[source], edge_send_sem.at[sep_at],
-            edge_recv_sem.at[source], front, sep_at,
-        )
+            place, place, edge_send_sem.at[sep_at], edge_recv_sem.at[source], front, sep_at
+        )
+
+    def edge_out(k):
+        sep_at = lax.rem(sep + k, n_sep)
+        return edge_copy(k, sep_at, sep, lax.rem(sep_at, 2))
+
+    def edge_in(k):
+        return edge_copy(n_sep - k, 0, lax.rem(sep + k, n_sep), core)
+
+    near = (1, n_sep - 1)
+    far = range(2, n_sep - 1)
+    for k in near:
+        edge_out(k).start()
 
     pair_g.wait_recv()
     summed = g_own[...] + pair_g_recv[...]
     g_own[...] = summed
-    g_send[...] = summed.astype(BF16)
-
-    def g_copy(z_at, source):
+    for part in range(PARTS):
+        g_send[part] = summed[part * hp : (part + 1) * hp].astype(BF16)
+
+    def g_copy(z_at, source, part):
         return to_device(
-            g_send, g_recv.at[source], g_send_sem.at[z_at], g_recv_sem.at[source],
-            front, 2 * z_at + core,
-        )
-
-    for k in range(1, n_sep):
-        edge_copy(lax.rem(sep + k, n_sep), sep).start()
-    for k in range(1, n_z):
-        g_copy(lax.rem(z + k, n_z), z).start()
+            g_send.at[part], g_recv.at[source, part], g_send_sem.at[z_at, part],
+            g_recv_sem.at[source, part], front, 2 * z_at + core,
+        )
+
+    for part in range(PARTS):
+        for k in range(1, n_z):
+            g_copy(lax.rem(z + k, n_z), z, part).start()
+        if part == 0:
+            for k in far:
+                edge_out(k).start()
 
     for one in loads[8:11]:
         one.wait()
@@ -271,19 +291,19 @@
 
     for one in loads[11:]:
         one.wait()
-    for k in range(1, n_sep):
-        edge_copy(0, lax.rem(sep + k, n_sep)).wait_recv()
-
-    sixteen = lax.broadcasted_iota(jnp.int32, (TILE, rank), 0)
+    for k in near:
+        edge_in(k).wait_recv()
+
+    sixteen = lax.broadcasted_iota(jnp.int32, (TILE, hr), 0)
     before_at = jnp.maximum(sep - 1, 0)
     after_at = jnp.minimum(sep + 1, n_sep - 1)
 
     def two_rows(height_at, first, second):
         return jnp.where(height_at == 0, first, jnp.where(height_at == 1, second, 0.0)).astype(BF16)
 
-    def neighbours(column):
-        before = edges[before_at, :, column * rank : (column + 1) * rank]
-        after = edges[after_at, :, (column + 1) * rank : (column + 2) * rank]
+    def neighbours(at, stride):
+        before = edges[before_at, :, at : at + hr]
+        after = edges[after_at, :, at + stride : at + stride + hr]
         return two_rows(
             sixteen, jnp.where(sep > 0, before, 0.0), jnp.where(sep < n_sep - 1, after, 0.0)
         )
@@ -298,7 +318,8 @@
             lax.broadcasted_iota(jnp.int32, (TILE, first.shape[1]), 0), first, last
         )
 
-    edge_left[...] = neighbours(4)
+    edge_left[:, :hr] = neighbours(8 * hr, rank)
+    edge_left[:, hr:] = neighbours(9 * hr, rank)
 
     def coef_copy(n):
         columns = pl.ds(n * quarter, quarter)
@@ -315,7 +336,8 @@
         ).astype(BF16)
         coef_copy(n).start()
 
-    edge_left[...] = neighbours(0)
+    edge_left[:, :hr] = neighbours(0, hr)
+    edge_left[:, hr:] = neighbours(6 * hr, hr)
     m_pair = to_device(m_send, m_recv, pair_send_sem.at[1], pair_recv_sem.at[1], front, sibling)
     for part, which, target in ((1, 1 - core, m_send), (0, core, m_own)):
         for n in range(2):
@@ -326,14 +348,16 @@
         if part == 1:
             m_pair.start()
 
-    own_lanes = half_at(core)
+    for k in far:
+        edge_in(k).wait_recv()
+    own_lanes = pl.multiple_of(core * 6 * hr, hr)
     for b in range(n_sep):
         if b < n_sep - 1:
             left = (
-                edges[b, :, pl.ds(own_lanes, hr)], edges[b + 1, :, pl.ds(rank + own_lanes, hr)],
+                edges[b, :, pl.ds(own_lanes, hr)], edges[b + 1, :, pl.ds(own_lanes + hr, hr)],
             )
             right = (
-                edges[b + 1, :, 3 * rank : 4 * rank], edges[b, :, 2 * rank : 3 * rank],
+                edges[b + 1, :, 2 * rank : 3 * rank], edges[b, :, rank : 2 * rank],
             )
         else:
             left = (jnp.zeros((1, hr), F32),) * 2
@@ -349,37 +373,41 @@
     for n in range(4):
         coef_copy(n).wait_recv()
     g_own[...] = total
-    for k in range(1, n_z):
-        source = lax.rem(z + k, n_z)
-        g_copy(0, source).wait_recv()
-        g_own[...] += g_recv[source].astype(F32)
-    negated = (-g_own[...]).astype(BF16)
-    g_twice[:, :rank] = negated
-    g_twice[:, rank:] = negated
-
     targets = (across, over, beyond)
 
-    def p_copy(n, j):
+    def p_copy(n, part, j):
         return to_device(
-            p_send.at[n, j], p_recv.at[n, j], p_send_sem.at[n, j], p_recv_sem.at[n, j],
-            targets[n], sep,
-        )
-
-    def piece(side_at, group_at, j):
-        at = pl.multiple_of(side_at * half + group_at * quarter + j * CW, CW)
-        return dot(g_twice[...], coef_l[:, pl.ds(at, CW)])
-
-    def m_piece(group_at, j):
-        return m_own[:, pl.ds(pl.multiple_of(group_at * quarter + j * CW, CW), CW)]
-
-    for j in range(n_top):
-        p_send[2, j] = piece(1 - side, 1 - group, j).astype(BF16)
-        p_copy(2, j).start()
-        p_send[1, j] = (piece(side, 1 - group, j) + m_piece(1 - group, j)).astype(BF16)
-        p_copy(1, j).start()
-        p_send[0, j] = piece(1 - side, group, j).astype(BF16)
-        p_copy(0, j).start()
-        own[2 * j] = piece(side, group, j) + m_piece(group, j)
+            p_send.at[n, part, j], p_recv.at[n, part, j], p_send_sem.at[n, part * n_top + j],
+            p_recv_sem.at[n, part * n_top + j], targets[n], sep,
+        )
+
+    for part in range(PARTS):
+        block = slice(part * hp, (part + 1) * hp)
+        for k in range(1, n_z):
+            source = lax.rem(z + k, n_z)
+            g_copy(0, source, part).wait_recv()
+            g_own[block, :] += g_recv[source, part].astype(F32)
+        negated = (-g_own[block, :]).astype(BF16)
+        g_twice[block, :rank] = negated
+        g_twice[block, rank:] = negated
+
+        def piece(side_at, group_at, j):
+            at = pl.multiple_of(side_at * half + group_at * quarter + j * CW, CW)
+            return dot(g_twice[block, :], coef_l[:, pl.ds(at, CW)])
+
+        def m_piece(group_at, j):
+            return m_own[block, pl.ds(pl.multiple_of(group_at * quarter + j * CW, CW), CW)]
+
+        for j in range(n_top):
+            p_send[2, part, j] = piece(1 - side, 1 - group, j).astype(BF16)
+            p_copy(2, part, j).start()
+            p_send[1, part, j] = (
+                piece(side, 1 - group, j) + m_piece(1 - group, j)
+            ).astype(BF16)
+            p_copy(1, part, j).start()
+            p_send[0, part, j] = piece(1 - side, group, j).astype(BF16)
+            p_copy(0, part, j).start()
+            own[part * pieces + 2 * j] = piece(side, group, j) + m_piece(group, j)
 
     @pl.when(sep > 0)
     def _():
@@ -405,28 +433,33 @@
             front, sep - 2,
         )
 
+    def place_of(i):
+        at = lax.rem(i, 2)
+        rest = lax.rem(i, pieces)
+        start = pl.multiple_of(core * hr + lax.div(i, pieces) * hp, hp)
+        return group + at - 2 * group * at, lax.div(rest, 2), pl.ds(start, hp)
+
     def final_copy(i):
-        at = lax.rem(i, 2)
-        place = coef_m.at[
-            group + at - 2 * group * at, lax.div(i, 2), :, pl.ds(half_at(core), hr)
-        ]
+        group_at, j, block = place_of(i)
+        place = coef_m.at[group_at, j, :, block]
         return to_device(
             place, place, final_send_sem.at[i], final_recv_sem.at[i], front, sibling
         )
 
     def gather(i):
-        j = lax.div(i, 2)
+        part = lax.div(i, pieces)
+        j = lax.div(lax.rem(i, pieces), 2)
 
         @pl.when(lax.rem(i, 2) == 0)
         def _():
-            p_copy(0, j).wait_recv()
-            own[i] += p_recv[0, j].astype(F32)
+            p_copy(0, part, j).wait_recv()
+            own[i] += p_recv[0, part, j].astype(F32)
 
         @pl.when(lax.rem(i, 2) == 1)
         def _():
-            p_copy(1, j).wait_recv()
-            p_copy(2, j).wait_recv()
-            own[i] = p_recv[1, j].astype(F32) + p_recv[2, j].astype(F32)
+            p_copy(1, part, j).wait_recv()
+            p_copy(2, part, j).wait_recv()
+            own[i] = p_recv[1, part, j].astype(F32) + p_recv[2, part, j].astype(F32)
 
     def prefix(i):
         @pl.when(z > 0)
@@ -452,15 +485,15 @@
         total = own[i] + right_recv[i].astype(F32) + left_recv[i].astype(F32)
         high = total.astype(BF16)
         low = (total - high.astype(F32)).astype(BF16)
-        at = lax.rem(i, 2)
-        group_at = group + at - 2 * group * at
-        coef_m[group_at, lax.div(i, 2), 0, pl.ds(half_at(core), hr)] = high
-        coef_m[group_at, lax.div(i, 2), 1, pl.ds(half_at(core), hr)] = low
+        group_at, j, block = place_of(i)
+        coef_m[group_at, j, 0, block] = high
+        coef_m[group_at, j, 1, block] = low
         final_copy(i).start()
 
     def top(j):
-        final_copy(2 * j).wait_recv()
-        final_copy(2 * j + 1).wait_recv()
+        for part in range(PARTS):
+            final_copy(part * pieces + 2 * j).wait_recv()
+            final_copy(part * pieces + 2 * j + 1).wait_recv()
         at = pl.multiple_of(j * CW, CW)
         taken = (
             dot(update_m[0], coef_m[0, j, 0]) + dot(update_m[1], coef_m[1, j, 0])
@@ -489,9 +522,9 @@
         on(t - z * HOP, items, prefix)
         on(t - (n_z - 1 - z) * HOP, items, suffix)
         on(t - last, items, final)
-        done = t - last - 1 - LAND
-
-        @pl.when(jnp.logical_and(done >= 0, jnp.logical_and(done < items, lax.rem(done, 2) == 0)))
+        done = t - last - 1 - LAND - (items - pieces)
+
+        @pl.when(jnp.logical_and(done >= 0, jnp.logical_and(done < pieces, lax.rem(done, 2) == 0)))
         def _():
             top(lax.div(done, 2))
 
@@ -503,14 +536,16 @@
     m_pair.wait_send()
     factor_copy.wait_send()
     for k in range(1, n_sep):
-        edge_copy(lax.rem(sep + k, n_sep), sep).wait_send()
-    for k in range(1, n_z):
-        g_copy(lax.rem(z + k, n_z), z).wait_send()
+        edge_out(k).wait_send()
+    for part in range(PARTS):
+        for k in range(1, n_z):
+            g_copy(lax.rem(z + k, n_z), z, part).wait_send()
     for n in range(4):
         coef_copy(n).wait_send()
     for n in range(3):
-        for j in range(n_top):
-            p_copy(n, j).wait_send()
+        for part in range(PARTS):
+            for j in range(n_top):
+                p_copy(n, part, j).wait_send()
 
     @pl.when(sep < n_sep - 1)
     def _():
@@ -543,14 +578,15 @@
     rank = operands[3].shape[2]
     half, quarter = width // 2, width // 4
     hr = rank // 2
+    hp = hr // PARTS
     n_top = quarter // CW
-    items = 2 * n_top
+    items = PARTS * 2 * n_top
     dma = pltpu.SemaphoreType.DMA
     hbm = pl.BlockSpec(memory_space=pltpu.HBM)
     vmem = pl.BlockSpec(memory_space=pltpu.VMEM)
     return pl.pallas_call(
         functools.partial(kernel, n_sep),
-        out_shape=jax.ShapeDtypeStruct((1, rows, quarter), F32),
+        out_shape=pltpu.VMEM((1, rows, quarter), F32),
         in_specs=[hbm] * 13,
         out_specs=vmem,
         scratch_shapes=[
@@ -577,20 +613,20 @@
             pltpu.VMEM((hr, rank), F32),
             pltpu.VMEM((hr, rank), F32),
             pltpu.VMEM((hr, rank), F32),
-            pltpu.VMEM((hr, rank), BF16),
-            pltpu.VMEM((n_sep // 2, hr, rank), BF16),
+            pltpu.VMEM((PARTS, hp, rank), BF16),
+            pltpu.VMEM((n_sep // 2, PARTS, hp, rank), BF16),
             pltpu.VMEM((hr, 2 * rank), BF16),
             pltpu.VMEM((2 * rank, width), BF16),
             pltpu.VMEM((hr, half), F32),
             pltpu.VMEM((hr, half), F32),
             pltpu.VMEM((hr, half), F32),
-            pltpu.VMEM((3, n_top, hr, CW), BF16),
-            pltpu.VMEM((3, n_top, hr, CW), BF16),
-            pltpu.VMEM((items, hr, CW), F32),
-            pltpu.VMEM((items, hr, CW), BF16),
-            pltpu.VMEM((items, hr, CW), BF16),
-            pltpu.VMEM((items, hr, CW), BF16),
-            pltpu.VMEM((items, hr, CW), BF16),
+            pltpu.VMEM((3, PARTS, n_top, hp, CW), BF16),
+            pltpu.VMEM((3, PARTS, n_top, hp, CW), BF16),
+            pltpu.VMEM((items, hp, CW), F32),
+            pltpu.VMEM((items, hp, CW), BF16),
+            pltpu.VMEM((items, hp, CW), BF16),
+            pltpu.VMEM((items, hp, CW), BF16),
+            pltpu.VMEM((items, hp, CW), BF16),
             pltpu.VMEM((2, n_top, 2, rank, CW), BF16),
             dma((13,)),
             dma((n_sep,)),
@@ -601,12 +637,12 @@
             dma((1,)),
             dma((2,)),
             dma((2,)),
-            dma((n_sep // 2,)),
-            dma((n_sep // 2,)),
+            dma((n_sep // 2, PARTS)),
+            dma((n_sep // 2, PARTS)),
             dma((4,)),
             dma((4,)),
-            dma((3, n_top)),
-            dma((3, n_top)),
+            dma((3, PARTS * n_top)),
+            dma((3, PARTS * n_top)),
             dma((items,)),
             dma((items,)),
             dma((items,)),
@@ -615,7 +651,7 @@
             dma((items,)),
         ],
         compiler_params=pltpu.CompilerParams(
-            collective_id=0, has_side_effects=True, vmem_limit_bytes=67043328
+            collective_id=0, has_side_effects=True, vmem_limit_bytes=57543328
         ),
     )(*operands)
 

time: 39.3 us -> 35.1 us (0.89)
  Pallas kernels: 35.5 us -> 32.7 us
  local copies, waits for them, and re-layouts: 2.06 us -> 0.88 us
    pallas_call x1, Pallas kernels: 35.5 us -> 32.7 us  [shards(): pl.pallas_call(functools.partial(kernel, n_sep), out_shape=pltpu.VMEM((1,...]
    unnamed x1, local copies, waits for them, and re-layouts: 2.06 us -> 0.88 us
where the time goes in v2:
time: 35.1 us; the launch traced here: 34.9 us
  Pallas kernels  32.7 us (93%)
  between operations  1.3 us (4%)
  local copies, waits for them, and re-layouts  0.88 us (3%)
    pallas_call x1, Pallas kernels, shards(): pl.pallas_call(functools.partial(kernel, n_sep), out_shape=pltpu.VMEM((1,...  32.7 us
    unnamed x1, local copies, waits for them, and re-layouts  0.88 us

profile of v2, /device:TPU:0, one launch (start us, length us, event | category | flops | bytes accessed | tf_op | source)
XLA Modules:
  0.0 34.9 jit_solution(3652614413488135070)
XLA Ops:
  1.3 32.7 %shard_map.127 = f32[1,512,384]{2,1,0:T(8,128)S(1)} custom-call(bf16[1,512,1536]{2,1,0:T(8,128)(2,1)} %rhs_leaf.1, bf16[1,512,768]{2,1,0:T(8,128)(2,1)} %rhs_middle.1, bf16[1,512,384]{2,1,0:T(8,128)(2,1)} %rhs_top.1, bf16[1,512,256]{2,1,0:T(8,128)(2,1)} %update_leaf.1, bf16[1,512,256]{2,1,0:T(8,128)(2,1)} %couple_leaf.1, bf16[1,512,256]{2,1,0:T(8,128)(2,1)} %update_middle.1, ...), custom_call_target="tpu_custom_call" | custom-call | tf_op jit(solution)/shard_map/pallas_call | solution.py:587
  34.0 0.9 %copy.15 = f32[1,512,384]{2,1,0:T(8,128)} copy(f32[1,512,384]{2,1,0:T(8,128)S(1)} %shard_map.127) | data formatting | bytes 1572864

commit v3 on v2

--- a/solution.py
+++ b/solution.py
@@ -12,7 +12,7 @@
 BF16 = jnp.bfloat16
 CW = 128
 PARTS = 2
-HOP = 5 * PARTS
+HOP = 12
 LAND = 2 * PARTS
 TILE = 16
 
@@ -41,7 +41,7 @@
     front_rows, rank_leaf, rank_middle, pivot_v, pivot_edge,
     leaf_v, middle_v, top_v, top_edge, couple_l, couple_m, update_l, update_m,
     weights, turned_l, turned_high, turned_low,
-    edges, edge_left, edge_right, pair_g_send, pair_g_recv, g_own, g_send, g_recv, g_twice,
+    edges, edge_left, edge_right, pair_g_send, pair_g_recv, g_own, g_send, g_recv, g_twice, product,
     coef_l, m_own, m_send, m_recv, p_send, p_recv, own,
     right_send, right_recv, left_send, left_recv, coef_m,
     load_sem, edge_send_sem, edge_recv_sem, tile_send_sem, tile_recv_sem,
@@ -209,7 +209,10 @@
     for which in range(2):
         scaled, full = weighed(couple_l, which, weights[0], rank_leaf_now)
         note((8 + which) * hr, rank, scaled)
-        turned_l[which * hr : (which + 1) * hr, :] = full.astype(BF16).T
+        turned = full.T
+        high = turned.astype(BF16)
+        turned_l[0, which * hr : (which + 1) * hr, :] = high
+        turned_l[1, which * hr : (which + 1) * hr, :] = (turned - high.astype(F32)).astype(BF16)
 
     def edge_copy(k, sep_at, source, core_at):
         place = edges.at[source]
@@ -331,7 +334,7 @@
     for n in range(4):
         columns = slice(n * quarter, (n + 1) * quarter)
         coef_l[0:rank, columns] = (
-            dot(turned_l[...], leaf_v[:, columns])
+            dot(turned_l[0], leaf_v[:, columns]) + dot(turned_l[1], leaf_v[:, columns])
             + dot_rows(edge_left[...], end_rows(leaf_v, 0, columns))
         ).astype(BF16)
         coef_copy(n).start()
@@ -387,27 +390,34 @@
             source = lax.rem(z + k, n_z)
             g_copy(0, source, part).wait_recv()
             g_own[block, :] += g_recv[source, part].astype(F32)
-        negated = (-g_own[block, :]).astype(BF16)
-        g_twice[block, :rank] = negated
-        g_twice[block, rank:] = negated
-
-        def piece(side_at, group_at, j):
-            at = pl.multiple_of(side_at * half + group_at * quarter + j * CW, CW)
-            return dot(g_twice[block, :], coef_l[:, pl.ds(at, CW)])
-
-        def m_piece(group_at, j):
-            return m_own[block, pl.ds(pl.multiple_of(group_at * quarter + j * CW, CW), CW)]
-
+        negated = -g_own[block, :]
+        high = negated.astype(BF16)
+        low = (negated - high.astype(F32)).astype(BF16)
+        for n in range(2):
+            lanes = slice(n * rank, (n + 1) * rank)
+            g_twice[part, :hp, lanes] = high
+            g_twice[part, hp:, lanes] = low
+
+        def multiply(side_at, slot):
+            at = pl.multiple_of(side_at * half, half)
+            both = dot(g_twice[part], coef_l[:, pl.ds(at, half)])
+            product[slot] = both[:hp] + both[hp:]
+
+        def piece(slot, group_at, j):
+            at = pl.multiple_of(group_at * quarter + j * CW, CW)
+            return product[slot, :, pl.ds(at, CW)]
+
+        multiply(1 - side, 0)
         for j in range(n_top):
-            p_send[2, part, j] = piece(1 - side, 1 - group, j).astype(BF16)
-            p_copy(2, part, j).start()
-            p_send[1, part, j] = (
-                piece(side, 1 - group, j) + m_piece(1 - group, j)
-            ).astype(BF16)
+            for n, group_at in ((2, 1 - group), (0, group)):
+                p_send[n, part, j] = piece(0, group_at, j).astype(BF16)
+                p_copy(n, part, j).start()
+        multiply(side, 1)
+        product[1] += m_own[block, :]
+        for j in range(n_top):
+            p_send[1, part, j] = piece(1, 1 - group, j).astype(BF16)
             p_copy(1, part, j).start()
-            p_send[0, part, j] = piece(1 - side, group, j).astype(BF16)
-            p_copy(0, part, j).start()
-            own[part * pieces + 2 * j] = piece(side, group, j) + m_piece(group, j)
+            own[part * pieces + 2 * j] = piece(1, group, j)
 
     @pl.when(sep > 0)
     def _():
@@ -441,7 +451,7 @@
 
     def final_copy(i):
         group_at, j, block = place_of(i)
-        place = coef_m.at[group_at, j, :, block]
+        place = coef_m.at[group_at, j, block]
         return to_device(
             place, place, final_send_sem.at[i], final_recv_sem.at[i], front, sibling
         )
@@ -486,8 +496,8 @@
         high = total.astype(BF16)
         low = (total - high.astype(F32)).astype(BF16)
         group_at, j, block = place_of(i)
-        coef_m[group_at, j, 0, block] = high
-        coef_m[group_at, j, 1, block] = low
+        coef_m[group_at, j, block, :CW] = high
+        coef_m[group_at, j, block, CW:] = low
         final_copy(i).start()
 
     def top(j):
@@ -495,10 +505,8 @@
             final_copy(part * pieces + 2 * j).wait_recv()
             final_copy(part * pieces + 2 * j + 1).wait_recv()
         at = pl.multiple_of(j * CW, CW)
-        taken = (
-            dot(update_m[0], coef_m[0, j, 0]) + dot(update_m[1], coef_m[1, j, 0])
-            + dot(update_m[0], coef_m[0, j, 1]) + dot(update_m[1], coef_m[1, j, 1])
-        )
+        both = dot(update_m[0], coef_m[0, j]) + dot(update_m[1], coef_m[1, j])
+        taken = both[:, :CW] + both[:, CW:]
         before = (
             top_edge[0, :, pl.ds(at, CW)].astype(F32)[TILE - 1 :]
             - taken[rows + TILE - 1 : rows + TILE]
@@ -604,7 +612,7 @@
             pltpu.VMEM((rows, rank), BF16),
             pltpu.VMEM((2, rows + 2 * TILE, rank), BF16),
             pltpu.VMEM((3, rows, CW), F32),
-            pltpu.VMEM((rank, rows), BF16),
+            pltpu.VMEM((2, rank, rows), BF16),
             pltpu.VMEM((rank, rows), BF16),
             pltpu.VMEM((rank, rows), BF16),
             pltpu.VMEM((n_sep, 1, 6 * rank), F32),
@@ -615,7 +623,8 @@
             pltpu.VMEM((hr, rank), F32),
             pltpu.VMEM((PARTS, hp, rank), BF16),
             pltpu.VMEM((n_sep // 2, PARTS, hp, rank), BF16),
-            pltpu.VMEM((hr, 2 * rank), BF16),
+            pltpu.VMEM((PARTS, 2 * hp, 2 * rank), BF16),
+            pltpu.VMEM((2, hp, half), F32),
             pltpu.VMEM((2 * rank, width), BF16),
             pltpu.VMEM((hr, half), F32),
             pltpu.VMEM((hr, half), F32),
@@ -627,7 +636,7 @@
             pltpu.VMEM((items, hp, CW), BF16),
             pltpu.VMEM((items, hp, CW), BF16),
             pltpu.VMEM((items, hp, CW), BF16),
-            pltpu.VMEM((2, n_top, 2, rank, CW), BF16),
+            pltpu.VMEM((2, n_top, rank, 2 * CW), BF16),
             dma((13,)),
             dma((n_sep,)),
             dma((n_sep,)),

time: 35.1 us -> 34.2 us (0.974)
  Pallas kernels: 32.7 us -> 31.9 us
    pallas_call x1, Pallas kernels: 32.7 us -> 31.9 us  [shards(): pl.pallas_call(functools.partial(kernel, n_sep), out_shape=pltpu.VMEM((1,...]
where the time goes in v3:
time: 34.2 us; the launch traced here: 34.1 us
  Pallas kernels  31.9 us (93%)
  between operations  1.3 us (4%)
  local copies, waits for them, and re-layouts  0.88 us (3%)
    pallas_call x1, Pallas kernels, shards(): pl.pallas_call(functools.partial(kernel, n_sep), out_shape=pltpu.VMEM((1,...  31.9 us
    unnamed x1, local copies, waits for them, and re-layouts  0.88 us

profile of v3, /device:TPU:0, one launch (start us, length us, event | category | flops | bytes accessed | tf_op | source)
XLA Modules:
  0.0 34.1 jit_solution(7290459449269001244)
XLA Ops:
  1.3 31.9 %shard_map.127 = f32[1,512,384]{2,1,0:T(8,128)S(1)} custom-call(bf16[1,512,1536]{2,1,0:T(8,128)(2,1)} %rhs_leaf.1, bf16[1,512,768]{2,1,0:T(8,128)(2,1)} %rhs_middle.1, bf16[1,512,384]{2,1,0:T(8,128)(2,1)} %rhs_top.1, bf16[1,512,256]{2,1,0:T(8,128)(2,1)} %update_leaf.1, bf16[1,512,256]{2,1,0:T(8,128)(2,1)} %couple_leaf.1, bf16[1,512,256]{2,1,0:T(8,128)(2,1)} %update_middle.1, ...), custom_call_target="tpu_custom_call" | custom-call | tf_op jit(solution)/shard_map/pallas_call | solution.py:595
  33.2 0.9 %copy.15 = f32[1,512,384]{2,1,0:T(8,128)} copy(f32[1,512,384]{2,1,0:T(8,128)S(1)} %shard_map.127) | data formatting | bytes 1572864

commit v4 on v3

--- a/solution.py
+++ b/solution.py
@@ -246,12 +246,11 @@
             g_recv_sem.at[source, part], front, 2 * z_at + core,
         )
 
+    for k in far:
+        edge_out(k).start()
     for part in range(PARTS):
         for k in range(1, n_z):
             g_copy(lax.rem(z + k, n_z), z, part).start()
-        if part == 0:
-            for k in far:
-                edge_out(k).start()
 
     for one in loads[8:11]:
         one.wait()

time: 34.2 us -> 33.9 us (level)
  no operation moved by 1% of the time
where the time goes in v4:
time: 33.9 us; the launch traced here: 33.8 us
  Pallas kernels  31.6 us (93%)
  between operations  1.3 us (4%)
  local copies, waits for them, and re-layouts  0.88 us (3%)
    pallas_call x1, Pallas kernels, shards(): pl.pallas_call(functools.partial(kernel, n_sep), out_shape=pltpu.VMEM((1,...  31.6 us
    unnamed x1, local copies, waits for them, and re-layouts  0.88 us

profile of v4, /device:TPU:0, one launch (start us, length us, event | category | flops | bytes accessed | tf_op | source)
XLA Modules:
  0.0 33.8 jit_solution(14816967590801438116)
XLA Ops:
  1.3 31.6 %shard_map.127 = f32[1,512,384]{2,1,0:T(8,128)S(1)} custom-call(bf16[1,512,1536]{2,1,0:T(8,128)(2,1)} %rhs_leaf.1, bf16[1,512,768]{2,1,0:T(8,128)(2,1)} %rhs_middle.1, bf16[1,512,384]{2,1,0:T(8,128)(2,1)} %rhs_top.1, bf16[1,512,256]{2,1,0:T(8,128)(2,1)} %update_leaf.1, bf16[1,512,256]{2,1,0:T(8,128)(2,1)} %couple_leaf.1, bf16[1,512,256]{2,1,0:T(8,128)(2,1)} %update_middle.1, ...), custom_call_target="tpu_custom_call" | custom-call | tf_op jit(solution)/shard_map/pallas_call | solution.py:594
  32.9 0.9 %copy.15 = f32[1,512,384]{2,1,0:T(8,128)} copy(f32[1,512,384]{2,1,0:T(8,128)S(1)} %shard_map.127) | data formatting | bytes 1572864
